TPU v7x, 32 devices: a whole 2x2x4 slice. The times are simulated.
32 devices in a mesh: seq: 8 (over z, x), exp: 4 (over y, core).
Axes of the slice: x: 2, y: 2, z: 4, core: 2. Of those that a mesh axis runs over, the one named last changes fastest.
Arguments:
- block_input: float32 [4096, 768], P(('seq', 'exp')), may hold values from -6 to 6
- seq_lengths: int32 [10], replicated, may hold values from 1 to 2048, 4096 in all
- expert_ids: int32 [4096, 1], P(('seq', 'exp')), may hold values from 0 to 3
- output_grad: float32 [4096, 768], P(('seq', 'exp')), may hold values from -6 to 6
- mixer_gain: float32 [768], replicated, may hold values from 0.5 to 1.5
- in_proj: float32 [768, 3072], replicated, may hold values from -0.21875 to 0.21875
- conv_weight: float32 [4, 1536], replicated, may hold values from -3 to 3
- conv_bias: float32 [1536], replicated, may hold values from -1.75 to 1.75
- state_proj: float32 [1536, 80], replicated, may hold values from -0.15625 to 0.15625
- step_proj: float32 [48, 1536], replicated, may hold values from -0.875 to 0.875
- step_bias: float32 [1536], replicated, may hold values from -7 to -2.5
- decay_log: float32 [1536, 16], replicated, may hold values from 0 to 2.77
- skip_gain: float32 [1536], replicated, may hold values from 0.5 to 1.5
- out_proj: float32 [1536, 768], replicated, may hold values from -0.3125 to 0.3125
- router_gain: float32 [768], replicated, may hold values from 0.5 to 1.5
- router: float32 [768, 4], replicated, may hold values from -0.15625 to 0.15625
- expert_up: float32 [4, 768, 3072], P('exp', None, 'seq'), may hold values from -0.21875 to 0.21875
- expert_down: float32 [4, 3072, 768], P('exp', 'seq'), may hold values from -0.875 to 0.875
Outputs:
- block_output: float32 [4096, 768], P(('seq', 'exp'))
- input_grad: float32 [4096, 768], P(('seq', 'exp'))
- grad_mixer_gain: float32 [768], replicated
- grad_in_proj: float32 [768, 3072], replicated
- grad_conv_weight: float32 [4, 1536], replicated
- grad_conv_bias: float32 [1536], replicated
- grad_state_proj: float32 [1536, 80], replicated
- grad_step_proj: float32 [48, 1536], replicated
- grad_step_bias: float32 [1536], replicated
- grad_decay_log: float32 [1536, 16], replicated
- grad_skip_gain: float32 [1536], replicated
- grad_out_proj: float32 [1536, 768], replicated
- grad_router_gain: float32 [768], replicated
- grad_router: float32 [768, 4], replicated
- grad_expert_up: float32 [4, 768, 3072], P('exp', None, 'seq')
- grad_expert_down: float32 [4, 3072, 768], P('exp', 'seq')
- expert_load: int32 [4], replicated
- dropped_load: int32 [4], replicated
All inputs are finite; a program needn't handle non-finite values.
Results may differ from a plain program's by a relative error of at most 0.0003.
Values sent between devices are 32-bit elements; how exact they have to be, the bound alone decides.
No kernel may reach another device: no remote copies, remote signals or barrier semaphores. Data moves between devices by JAX's collectives and lax.ppermute only.
A program may use at most 448 MiB of HBM per device.

v0:
```python
import jax
import jax.numpy as jnp
from jax import lax
from jax.sharding import PartitionSpec as P

precise = lax.Precision.HIGHEST
epsilon = 1e-05


def passed_along(block, axis, distance):
    devices = range(lax.axis_size(axis))
    route = [(i - distance, i) for i in devices if i - distance in devices]
    return lax.ppermute(block, axis, route)


def entering(value, axis, join, neutral, backward):
    count, mine = (lax.axis_size(axis), lax.axis_index(axis))
    pieces = jax.tree.map(lambda part: lax.all_gather(part, axis), value)
    if backward:
        pieces = jax.tree.map(lambda part: part[::-1], pieces)
        mine = count - 1 - mine
    so_far = jax.tree.map(
        lambda part, zero: jnp.full_like(part, 0) + jnp.asarray(zero, part.dtype), value, neutral
    )

    def lap(position, so_far):
        longer = join(so_far, jax.tree.map(lambda part: part[position], pieces))
        return jax.tree.map(lambda new, old: jnp.where(position < mine, new, old), longer, so_far)

    return lax.fori_loop(0, count - 1, lap, so_far)


def matmul_high(left, right):
    return jnp.dot(left, right, precision=precise, preferred_element_type=jnp.float32)


def rms_scale(values_in, gain):
    return (
        values_in
        * lax.rsqrt(jnp.mean(values_in * values_in, axis=1, keepdims=True) + epsilon)
        * gain
    )


def chain_states(earlier, later):
    return (later[0] * earlier[0], later[0] * earlier[1] + later[1])


def per_device(
    block_input,
    seq_lengths,
    expert_ids,
    output_grad,
    mixer_gain,
    in_proj,
    conv_weight,
    conv_bias,
    state_proj,
    step_proj,
    step_bias,
    decay_log,
    skip_gain,
    out_proj,
    router_gain,
    router,
    expert_up,
    expert_down,
):
    tokens_n = block_input.shape[0]
    kernel_taps = conv_weight.shape[0]
    inner_width = in_proj.shape[1] // 2
    low_rank = step_proj.shape[0]
    state_size = decay_log.shape[1]
    experts_n = router.shape[1]
    capacity = (5 * tokens_n + 4 * experts_n - 1) // (4 * experts_n)
    span_index = lax.axis_index(("seq", "exp"))
    span_first = span_index * tokens_n
    position = span_first + jnp.arange(tokens_n, dtype=jnp.int32)
    seq_starts = jnp.cumsum(seq_lengths) - seq_lengths
    before = seq_starts[None, :] <= position[:, None]
    own_start = jnp.max(jnp.where(before, seq_starts[None, :], 0), axis=1)
    fresh = (own_start == position).astype(jnp.float32)
    alive = (own_start < span_first).astype(jnp.float32)
    tap_pos = (
        position[:, None] - (kernel_taps - 1) + jnp.arange(kernel_taps, dtype=jnp.int32)[None, :]
    )
    tap_valid = (tap_pos >= own_start[:, None]).astype(jnp.float32)

    def project_in(block_input, mixer_gain, in_proj):
        joined = matmul_high(rms_scale(block_input, mixer_gain), in_proj)
        return (joined[:, :inner_width], joined[:, inner_width:])

    def conv_features(extended, conv_weight, conv_bias, state_proj, step_proj, step_bias):
        summed = jnp.broadcast_to(conv_bias[None, :], (tokens_n, inner_width))
        for offset in range(kernel_taps):
            summed = (
                summed
                + extended[offset : offset + tokens_n]
                * tap_valid[:, offset : offset + 1]
                * conv_weight[offset][None, :]
            )
        activated = jax.nn.silu(summed)
        projected = matmul_high(activated, state_proj)
        step_sizes = jax.nn.softplus(matmul_high(projected[:, :low_rank], step_proj) + step_bias)
        return (
            activated,
            step_sizes,
            projected[:, low_rank : low_rank + state_size],
            projected[:, low_rank + state_size :],
        )

    def scan_part(activated, step_sizes, in_state, out_state, decay_log):
        decay_rate = -jnp.exp(decay_log)
        block_len = min(32, tokens_n)
        blocks = tokens_n // block_len

        def advance(carried, pieces):
            act_b, step_b, in_b, out_b, fresh_b = pieces
            outputs = []
            for index in range(block_len):
                decay_now = jnp.exp(step_b[index][:, None] * decay_rate) * (1.0 - fresh_b[index])
                carried = (
                    decay_now * carried
                    + (step_b[index] * act_b[index])[:, None] * in_b[index][None, :]
                )
                outputs.append(jnp.sum(carried * out_b[index][None, :], axis=1))
            return (carried, jnp.stack(outputs))

        pieces = tuple(
            (
                member.reshape((blocks, block_len) + member.shape[1:])
                for member in (activated, step_sizes, in_state, out_state, fresh)
            )
        )
        zero_end, local_out = lax.scan(advance, jnp.zeros(decay_log.shape, jnp.float32), pieces)
        running_end = jnp.sum(step_sizes, axis=0)
        end_decay = jnp.exp(running_end[:, None] * decay_rate) * alive[tokens_n - 1]
        return (local_out.reshape(tokens_n, -1), zero_end, end_decay)

    def carry_terms(out_state, step_sizes, decay_log, start_state):
        decay_rate = -jnp.exp(decay_log)
        running = jnp.cumsum(step_sizes, axis=0)
        block_len = min(64, tokens_n)
        blocks = tokens_n // block_len

        def one_block(pieces):
            run_b, out_b, alive_b = pieces
            factor = jnp.exp(run_b[:, :, None] * decay_rate[None]) * start_state[None]
            return jnp.sum(factor * out_b[:, None, :], axis=2) * alive_b[:, None]

        shaped = (
            running.reshape(blocks, block_len, -1),
            out_state.reshape(blocks, block_len, -1),
            alive.reshape(blocks, block_len),
        )
        return lax.map(one_block, shaped).reshape(tokens_n, -1)

    def mixer_out(scan_out, activated, gate_z, skip_gain, out_proj, block_input):
        return block_input + matmul_high(
            (scan_out + skip_gain * activated) * jax.nn.silu(gate_z), out_proj
        )

    chosen = (expert_ids == jnp.arange(experts_n, dtype=jnp.int32)[None, :]).astype(jnp.float32)

    def route(resid, router_gain, router):
        normed_moe = rms_scale(resid, router_gain)
        probs = jax.nn.softmax(matmul_high(normed_moe, router), axis=1)
        return (normed_moe, jnp.sum(probs * chosen, axis=1))

    (inner_x, gate_z), proj_back = jax.vjp(project_in, block_input, mixer_gain, in_proj)
    previous = passed_along(inner_x[tokens_n - kernel_taps + 1 :], ("seq", "exp"), 1)
    extended = jnp.concatenate([previous, inner_x], axis=0)
    (activated, step_sizes, in_state, out_state), conv_back = jax.vjp(
        conv_features, extended, conv_weight, conv_bias, state_proj, step_proj, step_bias
    )
    (local_out, zero_end, end_decay), scan_back = jax.vjp(
        scan_part, activated, step_sizes, in_state, out_state, decay_log
    )
    identity_pair = (jnp.ones_like(end_decay), jnp.zeros_like(zero_end))
    start_state = entering(
        (end_decay, zero_end), ("seq", "exp"), chain_states, identity_pair, False
    )[1]
    correction, carry_back = jax.vjp(carry_terms, out_state, step_sizes, decay_log, start_state)
    scan_out = local_out + correction
    resid, mixer_back = jax.vjp(
        mixer_out, scan_out, activated, gate_z, skip_gain, out_proj, block_input
    )
    (normed_moe, gate), route_back = jax.vjp(route, resid, router_gain, router)
    ahead_count = jnp.cumsum(chosen, axis=0) - chosen
    slot_rank = jnp.sum(ahead_count * chosen, axis=1).astype(jnp.int32)
    kept = (slot_rank < capacity).astype(jnp.float32)
    slot_ids = expert_ids[:, 0] * capacity + slot_rank
    dispatch = (
        jnp.arange(experts_n * capacity, dtype=jnp.int32)[:, None] == slot_ids[None, :]
    ).astype(jnp.float32) * kept[None, :]
    buffer = matmul_high(dispatch, normed_moe).reshape(experts_n, capacity, -1)
    full_up, full_down = (
        lax.all_gather(expert_up, "seq", axis=2, tiled=True),
        lax.all_gather(expert_down, "seq", axis=1, tiled=True),
    )
    received = lax.all_to_all(buffer, "exp", split_axis=0, concat_axis=0, tiled=True)
    local_n = full_up.shape[0]
    items = received.shape[1]
    grouped = received.reshape(-1, local_n, items, received.shape[2])
    hidden_pre = jnp.einsum("secd,edf->secf", grouped, full_up, precision=precise)
    result = jnp.einsum("secf,efd->secd", jax.nn.gelu(hidden_pre), full_down, precision=precise)
    returned = lax.all_to_all(
        result.reshape(received.shape), "exp", split_axis=0, concat_axis=0, tiled=True
    )
    returned, received, hidden_pre = (
        returned,
        received,
        hidden_pre.reshape(received.shape[0], items, -1),
    )
    combined = jnp.einsum(
        "st,sd->td", dispatch, returned.reshape(experts_n * capacity, -1), precision=precise
    )
    block_output = resid + gate[:, None] * combined
    grad_gate = jnp.sum(output_grad * combined, axis=1)
    grad_back = jnp.einsum(
        "st,td->sd", dispatch, output_grad * gate[:, None], precision=precise
    ).reshape(experts_n, capacity, -1)
    grad_result = lax.all_to_all(grad_back, "exp", split_axis=0, concat_axis=0, tiled=True)
    use_up, use_down = (
        lax.all_gather(expert_up, "seq", axis=2, tiled=True),
        lax.all_gather(expert_down, "seq", axis=1, tiled=True),
    )
    local_n = use_up.shape[0]
    sources = grad_result.shape[0] // local_n
    grad_group = grad_result.reshape(sources, local_n, capacity, -1)
    hidden_group = hidden_pre.reshape(sources, local_n, capacity, -1)
    input_group = received.reshape(sources, local_n, capacity, -1)
    gelu_hidden, gelu_back = jax.vjp(jax.nn.gelu, hidden_group)
    grad_down_full = jnp.einsum("secf,secd->efd", gelu_hidden, grad_group, precision=precise)
    grad_hidden = gelu_back(jnp.einsum("secd,efd->secf", grad_group, use_down, precision=precise))[
        0
    ]
    grad_up_full = jnp.einsum("secd,secf->edf", input_group, grad_hidden, precision=precise)
    grad_received = jnp.einsum("secf,edf->secd", grad_hidden, use_up, precision=precise).reshape(
        grad_result.shape
    )
    grad_buffer = lax.all_to_all(grad_received, "exp", split_axis=0, concat_axis=0, tiled=True)
    grad_expert_up, grad_expert_down = (
        lax.psum_scatter(grad_up_full, "seq", scatter_dimension=2, tiled=True),
        lax.psum_scatter(grad_down_full, "seq", scatter_dimension=1, tiled=True),
    )
    grad_normed_moe = jnp.einsum(
        "st,sd->td", dispatch, grad_buffer.reshape(experts_n * capacity, -1), precision=precise
    )
    grad_resid_route, grad_router_gain, grad_router = route_back((grad_normed_moe, grad_gate))
    grad_resid = output_grad + grad_resid_route
    grad_scan, grad_act_mix, grad_gate_z, grad_skip_gain, grad_out_proj, grad_input_mix = (
        mixer_back(grad_resid)
    )
    grad_out_carry, grad_step_carry, grad_decay_carry, grad_start = carry_back(grad_scan)
    grad_end = entering((end_decay, grad_start), ("seq", "exp"), chain_states, identity_pair, True)[
        1
    ]
    grad_act_scan, grad_step_scan, grad_in_state, grad_out_scan, grad_decay_scan = scan_back(
        (grad_scan, grad_end, grad_end * start_state)
    )
    (
        grad_extended,
        grad_conv_weight,
        grad_conv_bias,
        grad_state_proj,
        grad_step_proj,
        grad_step_bias,
    ) = conv_back(
        (
            grad_act_mix + grad_act_scan,
            grad_step_carry + grad_step_scan,
            grad_in_state,
            grad_out_carry + grad_out_scan,
        )
    )
    edge_grad = passed_along(grad_extended[: kernel_taps - 1], ("seq", "exp"), -1)
    grad_inner = grad_extended[kernel_taps - 1 :] + jnp.concatenate(
        [jnp.zeros((tokens_n - kernel_taps + 1, inner_width), jnp.float32), edge_grad], axis=0
    )
    grad_input_proj, grad_mixer_gain, grad_in_proj = proj_back((grad_inner, grad_gate_z))
    input_grad = grad_input_mix + grad_input_proj
    grad_decay_log = grad_decay_carry + grad_decay_scan
    load_local = jnp.sum(chosen, axis=0)
    drop_local = jnp.sum(chosen * (1.0 - kept)[:, None], axis=0)
    summed_grads = lax.psum(
        (
            grad_mixer_gain,
            grad_in_proj,
            grad_conv_weight,
            grad_conv_bias,
            grad_state_proj,
            grad_step_proj,
            grad_step_bias,
            grad_decay_log,
            grad_skip_gain,
            grad_out_proj,
            grad_router_gain,
            grad_router,
            load_local,
            drop_local,
        ),
        ("seq", "exp"),
    )
    expert_load = summed_grads[12].astype(jnp.int32)
    dropped_load = summed_grads[13].astype(jnp.int32)
    return (
        block_output,
        input_grad,
        summed_grads[0],
        summed_grads[1],
        summed_grads[2],
        summed_grads[3],
        summed_grads[4],
        summed_grads[5],
        summed_grads[6],
        summed_grads[7],
        summed_grads[8],
        summed_grads[9],
        summed_grads[10],
        summed_grads[11],
        grad_expert_up,
        grad_expert_down,
        expert_load,
        dropped_load,
    )


def solution(mesh):
    in_specs = (
        P(("seq", "exp"), None),
        P(),
        P(("seq", "exp"), None),
        P(("seq", "exp"), None),
        P(),
        P(),
        P(),
        P(),
        P(),
        P(),
        P(),
        P(),
        P(),
        P(),
        P(),
        P(),
        P("exp", None, "seq"),
        P("exp", "seq", None),
    )
    out_specs = (
        P(("seq", "exp"), None),
        P(("seq", "exp"), None),
        P(),
        P(),
        P(),
        P(),
        P(),
        P(),
        P(),
        P(),
        P(),
        P(),
        P(),
        P(),
        P("exp", None, "seq"),
        P("exp", "seq", None),
        P(),
        P(),
    )
    return jax.shard_map(
        per_device, mesh=mesh, in_specs=in_specs, out_specs=out_specs, check_vma=False
    )
```

profile of v0, /device:TPU:0, one launch (start us, length us, event | category | flops | bytes accessed | tf_op | source)
XLA Modules:
  0.0 3072.7 jit_solution(16956716026353753182)
XLA Ops:
  36.6 739.4 %while.750 = (s32[]{:T(128)}, f32[1536,16]{0,1:T(8,128)S(1)}, f32[4,32,1536]{2,1,0:T(8,128)}, f32[4,1536,1]{1,2,0:T(1,128)}, f32[4,1536,16]{1,2,0:T(8,128)}, /*i...) while((s32[]{:T(128)}, f32[1536,16]{0,1:T(8,128)S(1)}, ...), condition=%wide.region_36.37_spmd.clone, body=%wide.region_3.36_spmd.clone.sunk | while | flops 11132994 | bytes 24794744 | solution.py:135
  785.7 52.7 %all-gather.15.cloned.1.call-done = f32[49152,16]{0,1:T(8,128)} async-done(((f32[1536,16]{0,1:T(8,128)}), f32[49152,16]{0,1:T(8,128)}) %all-gather.15.cloned.1.call-update) | async-done | bytes 3145744 | tf_op jit(solution)/shard_map/all_gather | solution.py:18
  843.9 56.0 %all-gather.13.cloned.1.call-done = f32[49152,16]{0,1:T(8,128)} async-done(((f32[1536,16]{0,1:T(8,128)}), f32[49152,16]{0,1:T(8,128)}) %all-gather.13.cloned.1.call-update) | async-done | bytes 3145744 | tf_op jit(solution)/shard_map/all_gather | solution.py:18
  903.7 68.8 %while.751 = (s32[]{:T(128)}, f32[1536,16]{0,1:T(8,128)S(1)}, s32[]{:T(128)}, f32[32,1536,16]{1,2,0:T(8,128)}, f32[32,1536,16]{1,0,2:T(8,128)}, /*index=5*/s32[]{:T(128)}, s32[]{:T(128)}) while((s32[]{:T(128)}, f32[1536,16]{0,1:T(8,128)S(1)}, s32[]{:T(128)}, f32[32,1536,16]{1,2,0:T(8,128)}, f32[32,1536,16]{1,0,2:T(8,128)}, ...), condition=%wide.region_40.41_spmd.clone, body=%wide.region_39.40_spmd.clone.sunk | while | flops 98308 | bytes 589929 | solution.py:30
  973.4 25.3 while.749
  1021.5 17.0 all-gather.9.cloned.1.call-done
  1046.9 129.9 %all-gather.11.cloned.1.call-done = f32[1,3072,768]{2,1,0:T(8,128)} async-done(((f32[1,384,768]{2,1,0:T(8,128)}), f32[1,3072,768]{2,1,0:T(8,128)}) %all-gather.11.cloned.1.call-update) | async-done | bytes 9437200 | tf_op jit(solution)/shard_map/all_gather | solution.py:199
  1204.4 11.1 all_to_all.20
  1215.5 13.0 fusion.598
  1229.9 13.1 fusion.582
  1258.2 9.3 multiply_reduce_fusion.131
  1269.1 23.9 while.752
  1299.4 15.4 reduce_window_sum.42
  1322.1 28.1 all-gather.17.cloned.1.call-done
  1363.7 68.2 %while.753 = (s32[]{:T(128)}, f32[1536,16]{0,1:T(8,128)S(1)}, s32[]{:T(128)}, f32[32,1536,16]{1,2,0:T(8,128)}, f32[32,1536,16]{1,0,2:T(8,128)}, /*index=5*/s32[]{:T(128)}, s32[]{:T(128)}) while((s32[]{:T(128)}, f32[1536,16]{0,1:T(8,128)S(1)}, s32[]{:T(128)}, f32[32,1536,16]{1,2,0:T(8,128)}, f32[32,1536,16]{1,0,2:T(8,128)}, ...), condition=%wide.region_60.61_spmd.clone, body=%wide.region_59.60_spmd.clone.sunk | while | flops 98308 | bytes 589929 | solution.py:30
  1435.2 710.6 %while.754 = (s32[]{:T(128)}, f32[1536,16]{0,1:T(8,128)}, f32[1536,16]{0,1:T(8,128)S(1)}, f32[4,32,1536]{2,1,0:T(8,128)}, f32[4,32,1536]{2,1,0:T(8,128)}, /*inde...) while((s32[]{:T(128)}, f32[1536,16]{0,1:T(8,128)}, ...), condition=%wide.region_190.191_spmd.clone, body=%wide.region_61.190_spmd.clone.sunk | while | flops 17356836 | bytes 57770112 | solution.py:135
  1464.6 13.3 multiply_reduce_fusion.200
  1507.0 15.2 multiply_reduce_fusion.201
  1642.2 13.3 multiply_reduce_fusion.200
  1684.4 15.2 multiply_reduce_fusion.201
  1819.7 13.3 multiply_reduce_fusion.200
  1862.1 15.2 multiply_reduce_fusion.201
  1996.8 13.3 multiply_reduce_fusion.200
  2039.2 15.2 multiply_reduce_fusion.201
  2160.5 10.1 fusion.603
  2172.2 10.4 convolution_bitcast_fusion
  2184.4 10.3 convolution_bitcast_fusion.1
  2196.3 12.1 multiply_reduce_fusion.137
  2208.5 44.7 %all-reduce.174 = (f32[768]{0:T(1024)}, f32[4,1536]{1,0:T(4,128)}, f32[1536]{0:T(1024)}, f32[1536]{0:T(1024)}, f32[1536]{0:T(1024)}, /*index=5*/f32[768]{0:T(102...) all-reduce(f32[768]{0:T(1024)S(1)} %get-tuple-element.12840, ...), channel_id=1, replica_groups=mesh['seq'=8,'exp'=4] {'seq','exp'}, use_global_device_ids=true, to_apply=%region_195.196 | all-reduce | flops 15368 | bytes 122944 | tf_op jit(solution)/shard_map/psum | solution.py:286
  2255.1 459.9 %all-reduce.178.cloned.1.call-done = (f32[768,3072]{1,0:T(8,128)}, f32[1536,80]{0,1:T(8,128)}, f32[48,1536]{1,0:T(8,128)}, f32[1536,16]{0,1:T(8,128)}, f32[1536,768]{1,0:T(8,128)}) async-done(((f32[768,3072]{1,0:T(8,128)}, f32[1536,80]{0,1:T(8,128)}, f32[48,1536]{1,0:T(8,128)}, f32[1536,16]{0,1:T(8,128)}, f32[1536,768]{1,0:T(8,128)}), (f32[768,3072]{1,0:T(8,128)}, f32[1536,80]{0,1:T(8,128)}, ...) | async-done | bytes 15040528 | tf_op jit(solution)/shard_map/psum | solution.py:286
  2715.1 170.9 %reduce-scatter.5.cloned.1.call-done = f32[1,384,768]{2,1,0:T(8,128)} async-done(((f32[1,3072,768]{2,1,0:T(8,128)}), f32[1,384,768]{2,1,0:T(8,128)}) %reduce-scatter.5.cloned.1.call-update) | async-done | bytes 1179664 | tf_op jit(solution)/shard_map/reduce_scatter | solution.py:245
  2885.9 166.6 %reduce-scatter.3.cloned.1.call-done = f32[1,768,384]{2,1,0:T(8,128)} async-done(((f32[1,768,3072]{2,1,0:T(8,128)}), f32[1,768,384]{2,1,0:T(8,128)}) %reduce-scatter.3.cloned.1.call-update) | async-done | bytes 1179664 | tf_op jit(solution)/shard_map/reduce_scatter | solution.py:244
  (3634 shorter events, 1617.0 us)
Async XLA Ops:
  7.2 831.3 %all-gather.15.cloned.1.call-start = ((), (), s32[]{:S(2)}) async-start(), calls=%async_computation.11 | async-start | bytes 3244032 | tf_op jit(solution)/shard_map/all_gather | solution.py:18
  16.8 9.4 collective-permute-start
  113.4 108.3 %copy-start.100 = (f32[4,32,16]{2,1,0:T(8,128)S(1)}, f32[4,32,16]{2,1,0:T(8,128)}, u32[]{:S(2)}) copy-start(f32[4,32,16]{2,1,0:T(8,128)} %copy-done.99) | copy-start | bytes 24580 | tf_op jit(solution)/shard_map/jvp()/while
  113.4 108.3 %copy-start.192 = (f32[4,1,16]{2,1,0:T(1,128)S(1)}, f32[4,1,16]{2,1,0:T(1,128)}, u32[]{:S(2)}) copy-start(f32[4,1,16]{2,1,0:T(1,128)} %copy-done.191) | copy-start | bytes 772 | tf_op jit(solution)/shard_map/jvp()/while
  117.0 104.5 %copy-start.205 = (f32[4]{0:T(128)}, f32[4]{0:T(128)S(1)}, u32[]{:S(2)}) copy-start(f32[4]{0:T(128)S(1)} %get-tuple-element.21621) | copy-start | bytes 52 | tf_op jit(solution)/shard_map/jvp()/while
  117.0 104.5 %copy-start.221 = (f32[4]{0:T(128)}, f32[4]{0:T(128)S(1)}, u32[]{:S(2)}) copy-start(f32[4]{0:T(128)S(1)} %get-tuple-element.21632) | copy-start | bytes 52 | tf_op jit(solution)/shard_map/jvp()/while
  298.1 108.3 %copy-start.100 = (f32[4,32,16]{2,1,0:T(8,128)S(1)}, f32[4,32,16]{2,1,0:T(8,128)}, u32[]{:S(2)}) copy-start(f32[4,32,16]{2,1,0:T(8,128)} %copy-done.99) | copy-start | bytes 24580 | tf_op jit(solution)/shard_map/jvp()/while
  298.1 108.3 %copy-start.192 = (f32[4,1,16]{2,1,0:T(1,128)S(1)}, f32[4,1,16]{2,1,0:T(1,128)}, u32[]{:S(2)}) copy-start(f32[4,1,16]{2,1,0:T(1,128)} %copy-done.191) | copy-start | bytes 772 | tf_op jit(solution)/shard_map/jvp()/while
  301.7 104.5 %copy-start.205 = (f32[4]{0:T(128)}, f32[4]{0:T(128)S(1)}, u32[]{:S(2)}) copy-start(f32[4]{0:T(128)S(1)} %get-tuple-element.21621) | copy-start | bytes 52 | tf_op jit(solution)/shard_map/jvp()/while
  301.7 104.5 %copy-start.221 = (f32[4]{0:T(128)}, f32[4]{0:T(128)S(1)}, u32[]{:S(2)}) copy-start(f32[4]{0:T(128)S(1)} %get-tuple-element.21632) | copy-start | bytes 52 | tf_op jit(solution)/shard_map/jvp()/while
  482.7 108.4 %copy-start.100 = (f32[4,32,16]{2,1,0:T(8,128)S(1)}, f32[4,32,16]{2,1,0:T(8,128)}, u32[]{:S(2)}) copy-start(f32[4,32,16]{2,1,0:T(8,128)} %copy-done.99) | copy-start | bytes 24580 | tf_op jit(solution)/shard_map/jvp()/while
  482.7 108.3 %copy-start.192 = (f32[4,1,16]{2,1,0:T(1,128)S(1)}, f32[4,1,16]{2,1,0:T(1,128)}, u32[]{:S(2)}) copy-start(f32[4,1,16]{2,1,0:T(1,128)} %copy-done.191) | copy-start | bytes 772 | tf_op jit(solution)/shard_map/jvp()/while
  486.3 104.6 %copy-start.205 = (f32[4]{0:T(128)}, f32[4]{0:T(128)S(1)}, u32[]{:S(2)}) copy-start(f32[4]{0:T(128)S(1)} %get-tuple-element.21621) | copy-start | bytes 52 | tf_op jit(solution)/shard_map/jvp()/while
  486.3 104.6 %copy-start.221 = (f32[4]{0:T(128)}, f32[4]{0:T(128)S(1)}, u32[]{:S(2)}) copy-start(f32[4]{0:T(128)S(1)} %get-tuple-element.21632) | copy-start | bytes 52 | tf_op jit(solution)/shard_map/jvp()/while
  486.4 104.5 %copy-start.225 = (f32[4]{0:T(128)}, f32[4]{0:T(128)S(1)}, u32[]{:S(2)}) copy-start(f32[4]{0:T(128)S(1)} %get-tuple-element.21642) | copy-start | bytes 52 | tf_op jit(solution)/shard_map/jvp()/while
  667.5 108.3 %copy-start.100 = (f32[4,32,16]{2,1,0:T(8,128)S(1)}, f32[4,32,16]{2,1,0:T(8,128)}, u32[]{:S(2)}) copy-start(f32[4,32,16]{2,1,0:T(8,128)} %copy-done.99) | copy-start | bytes 24580 | tf_op jit(solution)/shard_map/jvp()/while
  667.5 108.3 %copy-start.192 = (f32[4,1,16]{2,1,0:T(1,128)S(1)}, f32[4,1,16]{2,1,0:T(1,128)}, u32[]{:S(2)}) copy-start(f32[4,1,16]{2,1,0:T(1,128)} %copy-done.191) | copy-start | bytes 772 | tf_op jit(solution)/shard_map/jvp()/while
  671.1 104.5 %copy-start.205 = (f32[4]{0:T(128)}, f32[4]{0:T(128)S(1)}, u32[]{:S(2)}) copy-start(f32[4]{0:T(128)S(1)} %get-tuple-element.21621) | copy-start | bytes 52 | tf_op jit(solution)/shard_map/jvp()/while
  671.1 104.5 %copy-start.221 = (f32[4]{0:T(128)}, f32[4]{0:T(128)S(1)}, u32[]{:S(2)}) copy-start(f32[4]{0:T(128)S(1)} %get-tuple-element.21632) | copy-start | bytes 52 | tf_op jit(solution)/shard_map/jvp()/while
  776.7 123.1 %all-gather.13.cloned.1.call-start = ((), (), s32[]{:S(2)}) async-start(), calls=%async_computation.10 | async-start | bytes 3244032 | tf_op jit(solution)/shard_map/all_gather | solution.py:18
  777.4 261.1 %all-gather.9.cloned.1.call-start = ((), (), s32[]{:S(2)}) async-start(), calls=%async_computation.6 | async-start | bytes 10616832 | tf_op jit(solution)/shard_map/all_gather | solution.py:198
  778.2 398.6 %all-gather.11.cloned.1.call-start = ((), (), s32[]{:S(2)}) async-start(), calls=%async_computation.7 | async-start | bytes 10616832 | tf_op jit(solution)/shard_map/all_gather | solution.py:199
  1006.4 249.8 %copy-start.150 = (f32[128]{0:T(128)}, f32[128]{0:T(128)S(1)}, u32[]{:S(2)}) copy-start(f32[128]{0:T(128)S(1)} %fusion.679) | copy-start | bytes 1540
  1008.6 12.1 all-to-all-start
  1046.9 168.6 %copy-start.2 = (f32[4,1,40,3072]{3,2,0,1:T(8,128)}, f32[4,1,40,3072]{3,2,0,1:T(8,128)S(1)}, u32[]{:S(2)}) copy-start(f32[4,1,40,3072]{3,2,0,1:T(8,128)S(1)} %fusion.586) | copy-start | bytes 5898244
  1186.1 12.7 all-to-all-start.1
  1243.0 12.1 all-to-all-start.3
  1246.6 103.6 %all-gather.17.cloned.1.call-start = ((), (), s32[]{:S(2)}) async-start(), calls=%async_computation.12 | async-start | bytes 3244032 | tf_op jit(solution)/shard_map/all_gather | solution.py:18
  1293.7 1421.4 %all-reduce.178.cloned.1.call-start = ((), (), s32[]{:S(2)}) async-start(), calls=%async_computation.13 | async-start | bytes 30081024 | tf_op jit(solution)/shard_map/psum | solution.py:286
  2157.3 3.1 collective-permute-start.1
  2170.6 715.3 %reduce-scatter.5.cloned.1.call-start = ((), (), s32[]{:S(2)}) async-start(), calls=%async_computation.9 | async-start | bytes 10616832 | tf_op jit(solution)/shard_map/reduce_scatter | solution.py:245
  2182.7 869.9 %reduce-scatter.3.cloned.1.call-start = ((), (), s32[]{:S(2)}) async-start(), calls=%async_computation.8 | async-start | bytes 10616832 | tf_op jit(solution)/shard_map/reduce_scatter | solution.py:244
  (596 other events, 17580.3 us)
Sparse Core Ops, SparseCore 0:
  776.8 61.6 all-gather.14
  842.0 57.7 all-gather.12
  902.0 136.5 all-gather.8
  1040.6 136.1 all-gather.10
  1293.8 56.3 all-gather.16
  2170.8 544.2 all-reduce.177
  2721.2 164.7 reduce-scatter.4
  2890.1 162.3 reduce-scatter.2
where the time goes:
time: 3120 us; the launch traced here: 3070 us
  local copies, waits for them, and re-layouts  1110 us (36%)
  waiting for transfers between devices  1100 us (35%)
  other arithmetic  544 us (17%)
  matrix products  135 us (4%)
  loops' own time  92.2 us (3%)
  blocking collectives  55.8 us (2%)
    psum x1, waiting for transfers between devices, per_device(): lax.psum((grad_mixer_gain, grad_in_proj, grad_conv_weight, grad_conv_bias...  460 us
    dynamic_update_slice x388, local copies, waits for them, and re-layouts, scan_part(): lax.scan(advance, jnp.zeros(decay_log.shape, jnp.float32), pieces)  453 us
    dynamic_slice x324, local copies, waits for them, and re-layouts, scan_part(): lax.scan(advance, jnp.zeros(decay_log.shape, jnp.float32), pieces)  285 us
    reduce_scatter x1, waiting for transfers between devices, per_device(): lax.psum_scatter(grad_down_full, 'seq', scatter_dimension=1, tiled=True)  171 us
    reduce_scatter x1, waiting for transfers between devices, per_device(): lax.psum_scatter(grad_up_full, 'seq', scatter_dimension=2, tiled=True)  167 us
    all_gather x3, waiting for transfers between devices, entering(): pieces = jax.tree.map(lambda part: lax.all_gather(part, axis), value)  137 us
    all_gather x1, waiting for transfers between devices, per_device(): lax.all_gather(expert_down, 'seq', axis=1, tiled=True)  130 us
    mul x196, other arithmetic, advance(): step_b[index] * act_b[index]  128 us
  transfers between devices with their start and end apart: 13, of which 12 were waited for; matrix products, arithmetic and copies ran while one was open for 6% of the time, Pallas kernels for 0%

commit v1 on v0

--- a/solution.py
+++ b/solution.py
@@ -284,23 +284,26 @@
     load_local = jnp.sum(chosen, axis=0)
     drop_local = jnp.sum(chosen * (1.0 - kept)[:, None], axis=0)
     summed_grads = lax.psum(
-        (
-            grad_mixer_gain,
-            grad_in_proj,
-            grad_conv_weight,
-            grad_conv_bias,
-            grad_state_proj,
-            grad_step_proj,
-            grad_step_bias,
-            grad_decay_log,
-            grad_skip_gain,
-            grad_out_proj,
-            grad_router_gain,
-            grad_router,
-            load_local,
-            drop_local,
+        lax.psum(
+            (
+                grad_mixer_gain,
+                grad_in_proj,
+                grad_conv_weight,
+                grad_conv_bias,
+                grad_state_proj,
+                grad_step_proj,
+                grad_step_bias,
+                grad_decay_log,
+                grad_skip_gain,
+                grad_out_proj,
+                grad_router_gain,
+                grad_router,
+                load_local,
+                drop_local,
+            ),
+            "exp",
         ),
-        ("seq", "exp"),
+        "seq",
     )
     expert_load = summed_grads[12].astype(jnp.int32)
     dropped_load = summed_grads[13].astype(jnp.int32)

time: 3120 us -> 3320 us (1.064)
  waiting for transfers between devices: 1100 us -> 1280 us
    psum x0 -> x1, waiting for transfers between devices: none -> 471 us  [per_device(): lax.psum(lax.psum((grad_mixer_gain, grad_in_proj, grad_conv_weight, grad_...]
    psum x1, waiting for transfers between devices: 460 us -> 240 us  [per_device(): lax.psum((grad_mixer_gain, grad_in_proj, grad_conv_weight, grad_conv_bias...]
    reduce_scatter x1, waiting for transfers between devices: 171 us -> 99.6 us  [per_device(): lax.psum_scatter(grad_down_full, 'seq', scatter_dimension=1, tiled=True)]
    psum x0 -> x1, blocking collectives: none -> 42.3 us  [per_device(): lax.psum(lax.psum((grad_mixer_gain, grad_in_proj, grad_conv_weight, grad_...]
  transfers between devices with their start and end apart: 13 -> 14, of which waited for: 12 -> 13; matrix products, arithmetic and copies ran while one was open for 6% -> 6% of each run, Pallas kernels for 0% -> 0%
where the time goes in v1:
time: 3320 us; the launch traced here: 3270 us
  waiting for transfers between devices  1280 us (39%)
  local copies, waits for them, and re-layouts  1100 us (33%)
  other arithmetic  544 us (16%)
  matrix products  135 us (4%)
  loops' own time  103 us (3%)
  blocking collectives  65.1 us (2%)
    psum x1, waiting for transfers between devices, per_device(): lax.psum(lax.psum((grad_mixer_gain, grad_in_proj, grad_conv_weight, grad_...  471 us
    dynamic_update_slice x388, local copies, waits for them, and re-layouts, scan_part(): lax.scan(advance, jnp.zeros(decay_log.shape, jnp.float32), pieces)  453 us
    dynamic_slice x324, local copies, waits for them, and re-layouts, scan_part(): lax.scan(advance, jnp.zeros(decay_log.shape, jnp.float32), pieces)  285 us
    psum x1, waiting for transfers between devices, per_device(): lax.psum((grad_mixer_gain, grad_in_proj, grad_conv_weight, grad_conv_bias...  240 us
    reduce_scatter x1, waiting for transfers between devices, per_device(): lax.psum_scatter(grad_up_full, 'seq', scatter_dimension=2, tiled=True)  167 us
    all_gather x3, waiting for transfers between devices, entering(): pieces = jax.tree.map(lambda part: lax.all_gather(part, axis), value)  137 us
    all_gather x1, waiting for transfers between devices, per_device(): lax.all_gather(expert_down, 'seq', axis=1, tiled=True)  130 us
    mul x196, other arithmetic, advance(): step_b[index] * act_b[index]  128 us
  transfers between devices with their start and end apart: 14, of which 13 were waited for; matrix products, arithmetic and copies ran while one was open for 6% of the time, Pallas kernels for 0%

profile of v1, /device:TPU:0, one launch (start us, length us, event | category | flops | bytes accessed | tf_op | source)
XLA Modules:
  0.0 3271.8 jit_solution(10341354124014172786)
XLA Ops:
  36.6 749.6 %while.750 = (s32[]{:T(128)}, f32[1536,16]{0,1:T(8,128)S(1)}, f32[4,32,1536]{2,1,0:T(8,128)}, f32[4,1536,1]{1,2,0:T(1,128)}, f32[4,1536,16]{1,2,0:T(8,128)}, /*i...) while((s32[]{:T(128)}, f32[1536,16]{0,1:T(8,128)S(1)}, ...), condition=%wide.region_36.37_spmd.clone, body=%wide.region_3.36_spmd.clone.sunk | while | flops 11132994 | bytes 24794744 | solution.py:135
  795.8 52.8 %all-gather.15.cloned.1.call-done = f32[49152,16]{0,1:T(8,128)} async-done(((f32[1536,16]{0,1:T(8,128)}), f32[49152,16]{0,1:T(8,128)}) %all-gather.15.cloned.1.call-update) | async-done | bytes 3145744 | tf_op jit(solution)/shard_map/all_gather | solution.py:18
  854.0 56.0 %all-gather.13.cloned.1.call-done = f32[49152,16]{0,1:T(8,128)} async-done(((f32[1536,16]{0,1:T(8,128)}), f32[49152,16]{0,1:T(8,128)}) %all-gather.13.cloned.1.call-update) | async-done | bytes 3145744 | tf_op jit(solution)/shard_map/all_gather | solution.py:18
  913.8 68.8 %while.751 = (s32[]{:T(128)}, f32[1536,16]{0,1:T(8,128)S(1)}, s32[]{:T(128)}, f32[32,1536,16]{1,2,0:T(8,128)}, f32[32,1536,16]{1,0,2:T(8,128)}, /*index=5*/s32[]{:T(128)}, s32[]{:T(128)}) while((s32[]{:T(128)}, f32[1536,16]{0,1:T(8,128)S(1)}, s32[]{:T(128)}, f32[32,1536,16]{1,2,0:T(8,128)}, f32[32,1536,16]{1,0,2:T(8,128)}, ...), condition=%wide.region_40.41_spmd.clone, body=%wide.region_39.40_spmd.clone.sunk | while | flops 98308 | bytes 589929 | solution.py:30
  983.6 25.4 while.749
  1032.0 16.7 all-gather.9.cloned.1.call-done
  1057.1 129.9 %all-gather.11.cloned.1.call-done = f32[1,3072,768]{2,1,0:T(8,128)} async-done(((f32[1,384,768]{2,1,0:T(8,128)}), f32[1,3072,768]{2,1,0:T(8,128)}) %all-gather.11.cloned.1.call-update) | async-done | bytes 9437200 | tf_op jit(solution)/shard_map/all_gather | solution.py:199
  1214.5 11.0 all_to_all.20
  1225.6 13.0 fusion.598
  1239.9 13.1 fusion.582
  1279.2 24.0 while.752
  1309.9 15.4 reduce_window_sum.42
  1332.5 27.9 all-gather.17.cloned.1.call-done
  1373.9 68.2 %while.753 = (s32[]{:T(128)}, f32[1536,16]{0,1:T(8,128)S(1)}, s32[]{:T(128)}, f32[32,1536,16]{1,2,0:T(8,128)}, f32[32,1536,16]{1,0,2:T(8,128)}, /*index=5*/s32[]{:T(128)}, s32[]{:T(128)}) while((s32[]{:T(128)}, f32[1536,16]{0,1:T(8,128)S(1)}, s32[]{:T(128)}, f32[32,1536,16]{1,2,0:T(8,128)}, f32[32,1536,16]{1,0,2:T(8,128)}, ...), condition=%wide.region_60.61_spmd.clone, body=%wide.region_59.60_spmd.clone.sunk | while | flops 98308 | bytes 589929 | solution.py:30
  1445.4 710.2 %while.754 = (s32[]{:T(128)}, f32[1536,16]{0,1:T(8,128)}, f32[1536,16]{0,1:T(8,128)S(1)}, f32[4,32,1536]{2,1,0:T(8,128)}, f32[4,32,1536]{2,1,0:T(8,128)}, /*inde...) while((s32[]{:T(128)}, f32[1536,16]{0,1:T(8,128)}, ...), condition=%wide.region_190.191_spmd.clone, body=%wide.region_61.190_spmd.clone.sunk | while | flops 17356836 | bytes 57770112 | solution.py:135
  1474.6 13.2 multiply_reduce_fusion.200
  1516.9 15.3 multiply_reduce_fusion.201
  1652.0 13.2 multiply_reduce_fusion.200
  1694.1 15.3 multiply_reduce_fusion.201
  1829.4 13.2 multiply_reduce_fusion.200
  1871.7 15.3 multiply_reduce_fusion.201
  2006.3 13.2 multiply_reduce_fusion.200
  2048.7 15.3 multiply_reduce_fusion.201
  2170.3 10.1 fusion.603
  2182.0 10.7 convolution_bitcast_fusion
  2204.3 240.0 %all-reduce.183.cloned.1.call-done = (f32[768,3072]{1,0:T(8,128)}, f32[1536,80]{0,1:T(8,128)}, f32[48,1536]{1,0:T(8,128)}, f32[1536,16]{0,1:T(8,128)}, f32[1536,768]{1,0:T(8,128)}) async-done(((f32[768,3072]{1,0:T(8,128)}, f32[1536,80]{0,1:T(8,128)}, f32[48,1536]{1,0:T(8,128)}, f32[1536,16]{0,1:T(8,128)}, f32[1536,768]{1,0:T(8,128)}), (f32[768,3072]{1,0:T(8,128)}, f32[1536,80]{0,1:T(8,128)}, ...) | async-done | bytes 15040528 | tf_op jit(solution)/shard_map/psum | solution.py:287
  2446.0 12.2 multiply_reduce_fusion.137
  2458.2 11.7 all-reduce.176
  2470.0 42.3 %all-reduce.174 = (f32[768]{0:T(1024)}, f32[4,1536]{1,0:T(4,128)}, f32[1536]{0:T(1024)}, f32[1536]{0:T(1024)}, f32[1536]{0:T(1024)}, /*index=5*/f32[768]{0:T(102...) all-reduce(f32[768]{0:T(1024)S(1)} %get-tuple-element.14256, ...), channel_id=1, replica_groups=mesh['seq'=8,'exp'=4] {'seq'}, use_global_device_ids=true, to_apply=%region_196.197 | all-reduce | flops 15368 | bytes 122944 | tf_op jit(solution)/shard_map/psum | solution.py:286
  2514.2 99.6 %reduce-scatter.5.cloned.1.call-done = f32[1,384,768]{2,1,0:T(8,128)} async-done(((f32[1,3072,768]{2,1,0:T(8,128)}), f32[1,384,768]{2,1,0:T(8,128)}) %reduce-scatter.5.cloned.1.call-update) | async-done | bytes 1179664 | tf_op jit(solution)/shard_map/reduce_scatter | solution.py:245
  2613.8 167.2 %reduce-scatter.3.cloned.1.call-done = f32[1,768,384]{2,1,0:T(8,128)} async-done(((f32[1,768,3072]{2,1,0:T(8,128)}), f32[1,768,384]{2,1,0:T(8,128)}) %reduce-scatter.3.cloned.1.call-update) | async-done | bytes 1179664 | tf_op jit(solution)/shard_map/reduce_scatter | solution.py:244
  2780.9 471.0 %all-reduce.181.cloned.1.call-done = (f32[768,3072]{1,0:T(8,128)}, f32[1536,80]{0,1:T(8,128)}, f32[48,1536]{1,0:T(8,128)}, f32[1536,16]{0,1:T(8,128)}, f32[1536,768]{1,0:T(8,128)}) async-done(((f32[768,3072]{1,0:T(8,128)}, f32[1536,80]{0,1:T(8,128)}, f32[48,1536]{1,0:T(8,128)}, f32[1536,16]{0,1:T(8,128)}, f32[1536,768]{1,0:T(8,128)}), (f32[768,3072]{1,0:T(8,128)}, f32[1536,80]{0,1:T(8,128)}, ...) | async-done | bytes 15040528 | tf_op jit(solution)/shard_map/psum | solution.py:286
  (3638 shorter events, 1636.3 us)
Async XLA Ops:
  7.2 841.5 %all-gather.15.cloned.1.call-start = ((), (), s32[]{:S(2)}) async-start(), calls=%async_computation.11 | async-start | bytes 3244032 | tf_op jit(solution)/shard_map/all_gather | solution.py:18
  16.8 9.4 collective-permute-start
  123.3 108.3 %copy-start.100 = (f32[4,32,16]{2,1,0:T(8,128)S(1)}, f32[4,32,16]{2,1,0:T(8,128)}, u32[]{:S(2)}) copy-start(f32[4,32,16]{2,1,0:T(8,128)} %copy-done.99) | copy-start | bytes 24580 | tf_op jit(solution)/shard_map/jvp()/while
  123.3 108.3 %copy-start.192 = (f32[4,1,16]{2,1,0:T(1,128)S(1)}, f32[4,1,16]{2,1,0:T(1,128)}, u32[]{:S(2)}) copy-start(f32[4,1,16]{2,1,0:T(1,128)} %copy-done.191) | copy-start | bytes 772 | tf_op jit(solution)/shard_map/jvp()/while
  126.9 104.5 %copy-start.205 = (f32[4]{0:T(128)}, f32[4]{0:T(128)S(1)}, u32[]{:S(2)}) copy-start(f32[4]{0:T(128)S(1)} %get-tuple-element.21635) | copy-start | bytes 52 | tf_op jit(solution)/shard_map/jvp()/while
  126.9 104.5 %copy-start.221 = (f32[4]{0:T(128)}, f32[4]{0:T(128)S(1)}, u32[]{:S(2)}) copy-start(f32[4]{0:T(128)S(1)} %get-tuple-element.21646) | copy-start | bytes 52 | tf_op jit(solution)/shard_map/jvp()/while
  308.1 108.3 %copy-start.100 = (f32[4,32,16]{2,1,0:T(8,128)S(1)}, f32[4,32,16]{2,1,0:T(8,128)}, u32[]{:S(2)}) copy-start(f32[4,32,16]{2,1,0:T(8,128)} %copy-done.99) | copy-start | bytes 24580 | tf_op jit(solution)/shard_map/jvp()/while
  308.1 108.3 %copy-start.192 = (f32[4,1,16]{2,1,0:T(1,128)S(1)}, f32[4,1,16]{2,1,0:T(1,128)}, u32[]{:S(2)}) copy-start(f32[4,1,16]{2,1,0:T(1,128)} %copy-done.191) | copy-start | bytes 772 | tf_op jit(solution)/shard_map/jvp()/while
  311.7 104.5 %copy-start.205 = (f32[4]{0:T(128)}, f32[4]{0:T(128)S(1)}, u32[]{:S(2)}) copy-start(f32[4]{0:T(128)S(1)} %get-tuple-element.21635) | copy-start | bytes 52 | tf_op jit(solution)/shard_map/jvp()/while
  311.7 104.5 %copy-start.221 = (f32[4]{0:T(128)}, f32[4]{0:T(128)S(1)}, u32[]{:S(2)}) copy-start(f32[4]{0:T(128)S(1)} %get-tuple-element.21646) | copy-start | bytes 52 | tf_op jit(solution)/shard_map/jvp()/while
  492.8 108.4 %copy-start.100 = (f32[4,32,16]{2,1,0:T(8,128)S(1)}, f32[4,32,16]{2,1,0:T(8,128)}, u32[]{:S(2)}) copy-start(f32[4,32,16]{2,1,0:T(8,128)} %copy-done.99) | copy-start | bytes 24580 | tf_op jit(solution)/shard_map/jvp()/while
  492.8 108.3 %copy-start.192 = (f32[4,1,16]{2,1,0:T(1,128)S(1)}, f32[4,1,16]{2,1,0:T(1,128)}, u32[]{:S(2)}) copy-start(f32[4,1,16]{2,1,0:T(1,128)} %copy-done.191) | copy-start | bytes 772 | tf_op jit(solution)/shard_map/jvp()/while
  496.4 104.6 %copy-start.205 = (f32[4]{0:T(128)}, f32[4]{0:T(128)S(1)}, u32[]{:S(2)}) copy-start(f32[4]{0:T(128)S(1)} %get-tuple-element.21635) | copy-start | bytes 52 | tf_op jit(solution)/shard_map/jvp()/while
  496.4 104.6 %copy-start.221 = (f32[4]{0:T(128)}, f32[4]{0:T(128)S(1)}, u32[]{:S(2)}) copy-start(f32[4]{0:T(128)S(1)} %get-tuple-element.21646) | copy-start | bytes 52 | tf_op jit(solution)/shard_map/jvp()/while
  677.7 108.3 %copy-start.100 = (f32[4,32,16]{2,1,0:T(8,128)S(1)}, f32[4,32,16]{2,1,0:T(8,128)}, u32[]{:S(2)}) copy-start(f32[4,32,16]{2,1,0:T(8,128)} %copy-done.99) | copy-start | bytes 24580 | tf_op jit(solution)/shard_map/jvp()/while
  677.7 108.3 %copy-start.192 = (f32[4,1,16]{2,1,0:T(1,128)S(1)}, f32[4,1,16]{2,1,0:T(1,128)}, u32[]{:S(2)}) copy-start(f32[4,1,16]{2,1,0:T(1,128)} %copy-done.191) | copy-start | bytes 772 | tf_op jit(solution)/shard_map/jvp()/while
  681.3 104.5 %copy-start.205 = (f32[4]{0:T(128)}, f32[4]{0:T(128)S(1)}, u32[]{:S(2)}) copy-start(f32[4]{0:T(128)S(1)} %get-tuple-element.21635) | copy-start | bytes 52 | tf_op jit(solution)/shard_map/jvp()/while
  681.3 104.5 %copy-start.221 = (f32[4]{0:T(128)}, f32[4]{0:T(128)S(1)}, u32[]{:S(2)}) copy-start(f32[4]{0:T(128)S(1)} %get-tuple-element.21646) | copy-start | bytes 52 | tf_op jit(solution)/shard_map/jvp()/while
  786.9 123.1 %all-gather.13.cloned.1.call-start = ((), (), s32[]{:S(2)}) async-start(), calls=%async_computation.10 | async-start | bytes 3244032 | tf_op jit(solution)/shard_map/all_gather | solution.py:18
  787.6 261.1 %all-gather.9.cloned.1.call-start = ((), (), s32[]{:S(2)}) async-start(), calls=%async_computation.6 | async-start | bytes 10616832 | tf_op jit(solution)/shard_map/all_gather | solution.py:198
  788.4 398.6 %all-gather.11.cloned.1.call-start = ((), (), s32[]{:S(2)}) async-start(), calls=%async_computation.7 | async-start | bytes 10616832 | tf_op jit(solution)/shard_map/all_gather | solution.py:199
  1016.7 249.6 %copy-start.150 = (f32[128]{0:T(128)}, f32[128]{0:T(128)S(1)}, u32[]{:S(2)}) copy-start(f32[128]{0:T(128)S(1)} %fusion.679) | copy-start | bytes 1540
  1018.9 12.3 all-to-all-start
  1057.1 168.5 %copy-start.2 = (f32[4,1,40,3072]{3,2,0,1:T(8,128)}, f32[4,1,40,3072]{3,2,0,1:T(8,128)S(1)}, u32[]{:S(2)}) copy-start(f32[4,1,40,3072]{3,2,0,1:T(8,128)S(1)} %fusion.586) | copy-start | bytes 5898244
  1196.3 12.7 all-to-all-start.1
  1253.0 12.1 all-to-all-start.3
  1256.7 103.7 %all-gather.17.cloned.1.call-start = ((), (), s32[]{:S(2)}) async-start(), calls=%async_computation.12 | async-start | bytes 3244032 | tf_op jit(solution)/shard_map/all_gather | solution.py:18
  1303.9 1140.4 %all-reduce.183.cloned.1.call-start = ((), (), s32[]{:S(2)}) async-start(), calls=%async_computation.14 | async-start | bytes 30081024 | tf_op jit(solution)/shard_map/psum | solution.py:287
  2167.1 3.1 collective-permute-start.1
  2180.4 433.4 %reduce-scatter.5.cloned.1.call-start = ((), (), s32[]{:S(2)}) async-start(), calls=%async_computation.9 | async-start | bytes 10616832 | tf_op jit(solution)/shard_map/reduce_scatter | solution.py:245
  2192.7 588.2 %reduce-scatter.3.cloned.1.call-start = ((), (), s32[]{:S(2)}) async-start(), calls=%async_computation.8 | async-start | bytes 10616832 | tf_op jit(solution)/shard_map/reduce_scatter | solution.py:244
  2204.3 1047.7 %all-reduce.181.cloned.1.call-start = ((), (), s32[]{:S(2)}) async-start(), calls=%async_computation.13 | async-start | bytes 30081024 | tf_op jit(solution)/shard_map/psum | solution.py:286
  (597 other events, 17691.7 us)
Sparse Core Ops, SparseCore 0:
  787.0 61.6 all-gather.14
  852.2 57.7 all-gather.12
  912.2 136.5 all-gather.8
  1050.7 136.1 all-gather.10
  1304.0 56.3 all-gather.16
  2180.5 263.7 all-reduce.182
  2448.9 164.8 reduce-scatter.4
  2618.4 162.5 reduce-scatter.2
  2787.1 464.8 all-reduce.180
